TPU v7x, 128 devices: a whole 4x4x4 slice. The times are simulated.
128 devices in a mesh: seq: 8 (over z, core), exp: 16 (over x, y).
Axes of the slice: x: 4, y: 4, z: 4, core: 2. Of those that a mesh axis runs over, the one named last changes fastest.
Arguments:
- residual: bfloat16 [16384, 8192], P(('seq', 'exp')), may hold values from -6 to 6
- expert_rows: bfloat16 [8, 16, 16, 24, 8192], P('seq', 'exp'), may hold values from -6 to 6
- expert_ids: int32 [16384, 2], P(('seq', 'exp')), may hold values from 0 to 15, as said below
- expert_slots: int32 [16384, 2], P(('seq', 'exp')), may hold values from 0 to 23, as said below
- combine_weights: float32 [16384, 2], P(('seq', 'exp')), may hold values from 0.1 to 0.9
- norm_gain: float32 [8192], replicated, may hold values from 0.1 to 1.9
- in_weight: bfloat16 [8192, 8192], P(None, 'exp'), may hold values from -0.0625 to 0.0625
- conv_weight: float32 [4, 8192], P(None, 'exp'), may hold values from -3 to 3
- conv_bias: float32 [8192], P('exp'), may hold values from -0.5 to 0.5
- bc_weight: bfloat16 [8192, 128], P('exp'), may hold values from -0.00390625 to 0.00390625
- dt_weight: bfloat16 [8192, 128], P('exp'), may hold values from -0.0625 to 0.0625
- dt_bias: float32 [128], P('exp'), may hold values from -2 to 0.5
- decay_log: float32 [128], P('exp'), may hold values from -14 to -3.2
- skip_gain: float32 [128], P('exp'), may hold values from -1 to 3
Outputs:
- scan_output: bfloat16 [16384, 8192], P('seq', 'exp')
Inputs may be any that keep to these rules, and one draw needn't show every extreme that they name: `expert_ids`: A token's two ids differ. The tokens of one device name no expert more than 24 times, and in each span one expert is named exactly 24 times by the tokens of every device of the span. `expert_slots`: A token's slot at its k-th expert counts the earlier (token, k) pairs of the same device, in row-major order, that name the same expert.
All inputs are finite; a program needn't handle non-finite values.
Results may differ from a plain program's by a relative error of at most 0.0074.
Values may be sent and summed in bfloat16 or wider, within the bound.
No kernel may reach another device: no remote copies, remote signals or barrier semaphores. Data moves between devices by JAX's collectives and lax.ppermute only.
A program may use at most 320 MiB of HBM per device.

v0:
```python
import jax
import jax.numpy as jnp
from jax import lax
from jax.sharding import PartitionSpec as P

TOPK = 2
KCONV = 4
HEAD = 64
NSTATE = 64
STRETCH = 256


def passed_along(value, axis, steps):
    count = lax.axis_size(axis)
    leading, last = (max(0, -steps), min(count, count - steps))
    return lax.ppermute(value, axis, [(source, source + steps) for source in range(leading, last)])


def block_terms(b_rows, c_rows, steps_dt, decays, values):
    running = jnp.cumsum(decays, axis=0)
    scores = jnp.dot(c_rows, b_rows.T, preferred_element_type=jnp.float32)
    length = running.shape[0]
    causal = (jnp.arange(length)[:, None] >= jnp.arange(length)[None, :])[:, :, None]
    decay_gap = jnp.where(causal, running[:, None, :] - running[None, :, :], 0.0)
    mixing = jnp.where(
        causal, jnp.exp(decay_gap) * scores[:, :, None] * steps_dt[None, :, :], 0.0
    ).astype(jnp.bfloat16)
    inside = jnp.einsum("tsh,shp->thp", mixing, values, preferred_element_type=jnp.float32)
    carried = jnp.exp(running[-1][None, :] - running) * steps_dt
    states = jnp.einsum(
        "sn,shp->hnp",
        b_rows.astype(jnp.float32),
        carried[:, :, None] * values.astype(jnp.float32),
        precision=lax.Precision.HIGHEST,
    )
    return (running, inside, states, jnp.exp(running[-1]))


def shards(
    residual,
    expert_rows,
    expert_ids,
    expert_slots,
    combine_weights,
    norm_gain,
    in_weight,
    conv_weight,
    conv_bias,
    bc_weight,
    dt_weight,
    dt_bias,
    decay_log,
    skip_gain,
):
    own_rows, width = residual.shape
    returned = lax.all_to_all(expert_rows, "exp", split_axis=2, concat_axis=1, tiled=True)
    capacity = returned.shape[3]
    buffers = returned.reshape(returned.shape[1] * capacity, width)
    picked = jnp.take(buffers, expert_ids * capacity + expert_slots, axis=0)
    mixture = jnp.zeros((own_rows, width), jnp.float32)
    for column in range(TOPK):
        mixture = mixture + combine_weights[:, column][:, None] * picked[:, column].astype(
            jnp.float32
        )
    stream = residual.astype(jnp.float32) + mixture
    factor = lax.rsqrt(jnp.mean(stream * stream, axis=1, keepdims=True) + 1e-06)
    normed = (stream * factor * norm_gain[None, :]).astype(jnp.bfloat16)
    group_rows = own_rows * lax.axis_size("exp")
    local_width = in_weight.shape[1]
    x_in = jnp.dot(
        lax.all_gather(normed, "exp", axis=0, tiled=True),
        in_weight,
        preferred_element_type=jnp.float32,
    ).astype(jnp.bfloat16)
    rim_rows = passed_along(x_in[group_rows - (KCONV - 1) :], "seq", 1)
    padded = jnp.concatenate([rim_rows, x_in], axis=0)
    filtered = jnp.zeros((group_rows, local_width), jnp.float32) + conv_bias[None, :]
    for tap in range(KCONV):
        filtered = filtered + conv_weight[tap][None, :] * padded[tap : tap + group_rows].astype(
            jnp.float32
        )
    activated = jax.nn.silu(filtered).astype(jnp.bfloat16)
    state_part = jnp.dot(activated, bc_weight, preferred_element_type=jnp.float32)
    rate_part = jnp.dot(activated, dt_weight, preferred_element_type=jnp.float32)
    state_proj, dt_raw = lax.psum((state_part, rate_part), "exp")
    heads_here = local_width // HEAD
    first_head = lax.axis_index("exp") * heads_here
    steps_dt = jax.nn.softplus(
        lax.dynamic_slice_in_dim(dt_raw, first_head, heads_here, 1) + dt_bias[None, :]
    )
    decays = -jnp.exp(decay_log)[None, :] * steps_dt
    b_all = state_proj[:, :NSTATE].astype(jnp.bfloat16)
    c_all = state_proj[:, NSTATE:].astype(jnp.bfloat16)
    blocks = group_rows // STRETCH
    c_blocks = c_all.reshape(blocks, STRETCH, NSTATE)
    value_blocks = activated.reshape(blocks, STRETCH, heads_here, HEAD)

    def advance(carry, inputs):
        local_states, prefix_decay = carry
        b_rows, c_rows, block_dt, block_decays, values = inputs
        running, inside, states, total = block_terms(b_rows, c_rows, block_dt, block_decays, values)
        return (
            (total[:, None, None] * local_states + states, prefix_decay * total),
            (running, inside, local_states, prefix_decay),
        )

    start_carry = (
        jnp.zeros((heads_here, NSTATE, HEAD), jnp.float32),
        jnp.ones((heads_here,), jnp.float32),
    )
    (final_states, device_decay), (runnings, insides, starts, prefixes) = lax.scan(
        advance,
        start_carry,
        (
            b_all.reshape(blocks, STRETCH, NSTATE),
            c_blocks,
            steps_dt.reshape(blocks, STRETCH, heads_here),
            decays.reshape(blocks, STRETCH, heads_here),
            value_blocks,
        ),
    )
    empty_states = jnp.zeros((heads_here, NSTATE, HEAD), jnp.float32)

    def relay_turn(turn, carried):
        incoming, outgoing = carried
        incoming = passed_along(outgoing, "seq", 1)
        return (incoming, device_decay[:, None, None] * incoming + final_states)

    incoming, outgoing_last = lax.fori_loop(
        0, lax.axis_size("seq") - 1, relay_turn, (empty_states, final_states)
    )
    entering = starts + prefixes[:, :, None, None] * incoming[None]
    across = jnp.exp(runnings)[:, :, :, None] * jnp.einsum(
        "btn,bhnp->bthp", c_blocks.astype(jnp.float32), entering, precision=lax.Precision.HIGHEST
    )
    output = insides + across + skip_gain[None, None, :, None] * value_blocks.astype(jnp.float32)
    return output.astype(jnp.bfloat16).reshape(group_rows, local_width)


def solution(mesh):
    placed = (
        P(("seq", "exp"), None),
        P("seq", "exp", None, None, None),
        P(("seq", "exp"), None),
        P(("seq", "exp"), None),
        P(("seq", "exp"), None),
        P(),
        P(None, "exp"),
        P(None, "exp"),
        P("exp"),
        P("exp", None),
        P("exp", None),
        P("exp"),
        P("exp"),
        P("exp"),
    )
    return jax.shard_map(
        shards, mesh=mesh, in_specs=placed, out_specs=P("seq", "exp"), check_vma=False
    )
```

profile of v0, /device:TPU:1, one launch (start us, length us, event | category | flops | bytes accessed | tf_op | source)
XLA Modules:
  0.0 613.9 jit_solution(3130771036729045118)
XLA Ops:
  6.5 7.8 %all-to-all-start = ((bf16[1,1,16,24,8192]{4,3,1,0,2:T(8,128)(2,1)}), bf16[1,1,16,24,8192]{4,3,1,0,2:T(8,128)(2,1)}, u32[]{:S(2)}, u32[]{:S(2)}) async-start(bf16[1,1,16,24,8192]{4,3,1,0,2:T(8,128)(2,1)} %bitcast.113), calls=%async_computation | async-start | bytes 12582912 | tf_op jit(solution)/shard_map/all_to_all | solution.py:56
  14.7 100.4 %all-to-all-done = bf16[1,1,16,24,8192]{4,3,1,0,2:T(8,128)(2,1)} async-done(((bf16[1,1,16,24,8192]{4,3,1,0,2:T(8,128)(2,1)}), bf16[1,1,16,24,8192]{4,3,1,0,2:T(8,128)(2,1)}, u32[]{:S(2)}, u32[]{:S(2)}) %all-to-all-start) | async-done | bytes 6291488 | tf_op jit(solution)/shard_map/all_to_all | solution.py:56
  115.1 12.6 %gather_fusion = bf16[256,8192]{1,0:T(8,128)(2,1)} fusion(bf16[384,8192]{1,0:T(8,128)(2,1)} %bitcast.3, s32[1024]{0:T(1024)S(1)} %pad_clamp_fusion), kind=kCustom, calls=%fused_computation | custom fusion | bytes 8389632 | tf_op jit(solution)/shard_map/jit(_take)/gather | solution.py:59
  127.7 7.6 %reshape.94 = bf16[128,2,8192]{2,1,0:T(2,128)(2,1)} reshape(bf16[256,8192]{1,0:T(8,128)(2,1)} %gather_fusion) | data formatting | bytes 8388608 | tf_op jit(solution)/shard_map/jit(_take)/gather | solution.py:59
  135.3 7.2 %copy_select_fusion = bf16[128,2,8192]{2,0,1:T(8,128)(2,1)S(1)} fusion(bf16[128,2,8192]{2,1,0:T(2,128)(2,1)} %reshape.94, pred[128,2]{0,1:T(4,128)(4,1)S(1)} %get-tuple-element.250), kind=kLoop, calls=%fused_computation.47 | loop fusion | flops 2097152 | bytes 8388864 | tf_op jit(solution)/shard_map/jit(_take)/select_n | solution.py:59
  142.6 1.4 multiply_reduce_fusion
  144.0 3.0 multiply_convert_fusion.1
  147.1 205.3 %all-gather.2.cloned.1.call-done = bf16[2048,8192]{1,0:T(8,128)(2,1)} async-done(((bf16[128,8192]{1,0:T(8,128)(2,1)}), bf16[2048,8192]{1,0:T(8,128)(2,1)}) %all-gather.2.cloned.1.call-update) | async-done | bytes 33554448 | tf_op jit(solution)/shard_map/all_gather | solution.py:71
  352.4 23.7 %convolution_convert_fusion = bf16[2048,512]{1,0:T(8,128)(2,1)S(1)} fusion(bf16[2048,8192]{1,0:T(8,128)(2,1)} %all-gather.2.cloned.1.call-done, bf16[8192,512]{1,0:T(8,128)(2,1)} %param.24), kind=kOutput, calls=%fused_computation.52 | convolution fusion | flops 17180917760 | bytes 44040192 | tf_op jit(solution)/shard_map/dot_general | solution.py:70
  376.2 1.3 copy-done.4
  377.5 3.7 collective-permute-start.1
  382.0 6.0 multiply_convert_fusion
  388.0 1.8 fusion.34
  389.8 1.7 fusion.35
  391.5 3.6 reshape.109
  395.2 4.0 copy.57
  399.2 75.3 %all-reduce.4 = bf16[2048,128]{1,0:T(8,128)(2,1)S(1)} all-reduce(f32[2048,128]{1,0:T(8,128)} %fusion.35), channel_id=1, replica_groups=mesh['seq'=8,'exp'=16] {'exp'}, use_global_device_ids=true, to_apply=%region_1.2 | all-reduce | flops 262144 | bytes 1572864 | tf_op jit(solution)/shard_map/psum | solution.py:85
  475.5 1.2 copy.58
  477.9 38.5 %while.34 = (s32[]{:T(128)}, f32[8,64,64]{1,2,0:T(8,128)S(1)}, f32[8]{0:T(128)S(1)}, f32[8,256,8]{1,2,0:T(8,128)}, f32[8,256,8,64]{1,3,2,0:T(8,128)}, /*index=5*...) while((s32[]{:T(128)}, f32[8,64,64]{1,2,0:T(8,128)S(1)}, ...), condition=%wide.region_6.7_spmd.clone, body=%wide.region_3.6_spmd.clone.sunk | while | flops 180033568 | bytes 2758157 | solution.py:111
  479.3 1.6 fusion.62
  484.1 1.6 fusion.62
  488.9 1.6 fusion.62
  493.7 1.6 fusion.62
  498.5 1.6 fusion.62
  503.3 1.6 fusion.62
  508.1 1.6 fusion.62
  513.0 1.5 fusion.62
  516.6 71.0 %while.33 = (s32[]{:T(128)}, f32[8,64,64]{2,1,0:T(8,128)}, f32[8,64,64]{2,1,0:T(8,128)S(1)}, f32[8]{0:T(128)S(1)}, f32[8,64,64]{2,1,0:T(8,128)S(1)}, /*index=5*/s32[]{:T(128)}) while((s32[]{:T(128)}, f32[8,64,64]{2,1,0:T(8,128)}, f32[8,64,64]{2,1,0:T(8,128)S(1)}, f32[8]{0:T(128)S(1)}, f32[8,64,64]{2,1,0:T(8,128)S(1)}, ...), condition=%wide.region_8.9_spmd, body=%wide.region_7.8_spmd.sunk | while | flops 65538 | bytes 1441961 | solution.py:129
  516.6 16.7 %collective-permute-start = (f32[8,64,64]{2,1,0:T(8,128)S(1)}, f32[8,64,64]{2,1,0:T(8,128)S(1)}, u32[]{:S(2)}, u32[]{:S(2)}) collective-permute-start(f32[8,64,64]{2,1,0:T(8,128)S(1)} %get-tuple-element.428), channel_id=1, source_target_pairs={{0,16},{16,32},{32,48},{48,64},{64,80},{80,96},{96,112},{1,17},{17... | collective-permute-start | bytes 393224 | tf_op jit(solution)/shard_map/while/body/eval_jaxpr/ppermute | solution.py:16
  533.3 3.3 collective-permute-done
  537.3 4.4 collective-permute-start
  541.7 3.3 collective-permute-done
  545.7 4.4 collective-permute-start
  550.1 3.3 collective-permute-done
  554.1 4.4 collective-permute-start
  558.5 3.3 collective-permute-done
  562.5 4.4 collective-permute-start
  566.8 3.3 collective-permute-done
  570.8 4.4 collective-permute-start
  575.2 3.3 collective-permute-done
  579.2 4.4 collective-permute-start
  583.6 3.3 collective-permute-done
  587.6 1.1 copy.61
  588.7 1.8 multiply_add_fusion.1
  590.5 1.8 fusion.36
  592.7 2.8 add_convert_fusion
  595.6 5.1 copy.67
  600.6 6.4 %reshape.108 = bf16[2048,512]{1,0:T(8,128)(2,1)} reshape(bf16[8,256,8,64]{3,2,1,0:T(8,128)(2,1)} %copy.67) | data formatting | bytes 4194304 | tf_op jit(solution)/shard_map/reshape | solution.py:137
  (197 shorter events, 34.4 us)
Async XLA Ops:
  6.5 381.5 %copy-start = (bf16[512,128]{1,0:T(8,128)(2,1)S(1)}, bf16[512,128]{1,0:T(8,128)(2,1)}, u32[]{:S(2)}) copy-start(bf16[512,128]{1,0:T(8,128)(2,1)} %param.28) | copy-start | bytes 393220
  6.5 7.8 %copy-start.10 = (s32[128,2]{0,1:T(2,128)S(1)}, s32[128,2]{0,1:T(2,128)}, u32[]{:S(2)}) copy-start(s32[128,2]{0,1:T(2,128)} %param.21) | copy-start | bytes 3076
  6.5 7.8 %copy-start.11 = (s32[128,2]{0,1:T(2,128)S(1)}, s32[128,2]{0,1:T(2,128)}, u32[]{:S(2)}) copy-start(s32[128,2]{0,1:T(2,128)} %param.20) | copy-start | bytes 3076
  6.5 8.1 %copy-start.12 = (f32[128,2]{0,1:T(2,128)S(1)}, f32[128,2]{0,1:T(2,128)}, u32[]{:S(2)}) copy-start(f32[128,2]{0,1:T(2,128)} %param.22) | copy-start | bytes 3076
  6.5 108.6 %all-to-all-start = ((bf16[1,1,16,24,8192]{4,3,1,0,2:T(8,128)(2,1)}), bf16[1,1,16,24,8192]{4,3,1,0,2:T(8,128)(2,1)}, u32[]{:S(2)}, u32[]{:S(2)}) async-start(bf16[1,1,16,24,8192]{4,3,1,0,2:T(8,128)(2,1)} %bitcast.113), calls=%async_computation | async-start | bytes 12582912 | tf_op jit(solution)/shard_map/all_to_all | solution.py:56
  14.3 338.1 %all-gather.2.cloned.1.call-start = ((), (), s32[]{:S(2)}) async-start(), calls=%async_computation.1 | async-start | bytes 35651584 | tf_op jit(solution)/shard_map/all_gather | solution.py:71
  135.3 7.2 %copy-start.2 = (bf16[128,8192]{1,0:T(8,128)(2,1)S(1)}, bf16[128,8192]{1,0:T(8,128)(2,1)}, u32[]{:S(2)}) copy-start(bf16[128,8192]{1,0:T(8,128)(2,1)} %param.18) | copy-start | bytes 6291460
  142.5 1.4 copy-start.7
  144.0 3.1 copy-start.8
  147.0 330.0 %all-reduce.3.cloned.1.call-start = ((), (), s32[]{:S(2)}) async-start(), calls=%async_computation.2 | async-start | bytes 2097152 | tf_op jit(solution)/shard_map/psum | solution.py:85
  147.1 234.2 %copy-start.15 = (f32[8]{0:T(128)S(1)}, f32[8]{0:T(128)}, u32[]{:S(2)}) copy-start(f32[8]{0:T(128)} %param.30) | copy-start | bytes 100
  147.1 234.9 %copy-start.9 = (f32[512]{0:T(512)S(1)}, f32[512]{0:T(512)}, u32[]{:S(2)}) copy-start(f32[512]{0:T(512)} %param.26) | copy-start | bytes 6148
  376.2 1.3 copy-start.4
  377.5 4.5 collective-permute-start.1
  382.0 7.8 %copy-start.5 = (bf16[512,128]{1,0:T(8,128)(2,1)S(1)}, bf16[512,128]{1,0:T(8,128)(2,1)}, u32[]{:S(2)}) copy-start(bf16[512,128]{1,0:T(8,128)(2,1)} %param.27) | copy-start | bytes 393220
  395.2 81.8 %copy-start.13 = (f32[8]{0:T(128)S(1)}, f32[8]{0:T(128)}, u32[]{:S(2)}) copy-start(f32[8]{0:T(128)} %param.29) | copy-start | bytes 100
  516.6 20.0 %collective-permute-start = (f32[8,64,64]{2,1,0:T(8,128)S(1)}, f32[8,64,64]{2,1,0:T(8,128)S(1)}, u32[]{:S(2)}, u32[]{:S(2)}) collective-permute-start(f32[8,64,64]{2,1,0:T(8,128)S(1)} %get-tuple-element.428), channel_id=1, source_target_pairs={{0,16},{16,32},{32,48},{48,64},{64,80},{80,96},{96,112},{1,17},{17... | collective-permute-start | bytes 393224 | tf_op jit(solution)/shard_map/while/body/eval_jaxpr/ppermute | solution.py:16
  536.6 0.7 copy-start.1
  537.3 7.7 %collective-permute-start = (f32[8,64,64]{2,1,0:T(8,128)S(1)}, f32[8,64,64]{2,1,0:T(8,128)S(1)}, u32[]{:S(2)}, u32[]{:S(2)}) collective-permute-start(f32[8,64,64]{2,1,0:T(8,128)S(1)} %get-tuple-element.428), channel_id=1, source_target_pairs={{0,16},{16,32},{32,48},{48,64},{64,80},{80,96},{96,112},{1,17},{17... | collective-permute-start | bytes 393224 | tf_op jit(solution)/shard_map/while/body/eval_jaxpr/ppermute | solution.py:16
  545.0 0.7 copy-start.1
  545.7 7.7 %collective-permute-start = (f32[8,64,64]{2,1,0:T(8,128)S(1)}, f32[8,64,64]{2,1,0:T(8,128)S(1)}, u32[]{:S(2)}, u32[]{:S(2)}) collective-permute-start(f32[8,64,64]{2,1,0:T(8,128)S(1)} %get-tuple-element.428), channel_id=1, source_target_pairs={{0,16},{16,32},{32,48},{48,64},{64,80},{80,96},{96,112},{1,17},{17... | collective-permute-start | bytes 393224 | tf_op jit(solution)/shard_map/while/body/eval_jaxpr/ppermute | solution.py:16
  553.4 0.7 copy-start.1
  554.1 7.7 %collective-permute-start = (f32[8,64,64]{2,1,0:T(8,128)S(1)}, f32[8,64,64]{2,1,0:T(8,128)S(1)}, u32[]{:S(2)}, u32[]{:S(2)}) collective-permute-start(f32[8,64,64]{2,1,0:T(8,128)S(1)} %get-tuple-element.428), channel_id=1, source_target_pairs={{0,16},{16,32},{32,48},{48,64},{64,80},{80,96},{96,112},{1,17},{17... | collective-permute-start | bytes 393224 | tf_op jit(solution)/shard_map/while/body/eval_jaxpr/ppermute | solution.py:16
  561.8 0.7 copy-start.1
  562.5 7.7 %collective-permute-start = (f32[8,64,64]{2,1,0:T(8,128)S(1)}, f32[8,64,64]{2,1,0:T(8,128)S(1)}, u32[]{:S(2)}, u32[]{:S(2)}) collective-permute-start(f32[8,64,64]{2,1,0:T(8,128)S(1)} %get-tuple-element.428), channel_id=1, source_target_pairs={{0,16},{16,32},{32,48},{48,64},{64,80},{80,96},{96,112},{1,17},{17... | collective-permute-start | bytes 393224 | tf_op jit(solution)/shard_map/while/body/eval_jaxpr/ppermute | solution.py:16
  570.1 0.7 copy-start.1
  570.8 7.7 %collective-permute-start = (f32[8,64,64]{2,1,0:T(8,128)S(1)}, f32[8,64,64]{2,1,0:T(8,128)S(1)}, u32[]{:S(2)}, u32[]{:S(2)}) collective-permute-start(f32[8,64,64]{2,1,0:T(8,128)S(1)} %get-tuple-element.428), channel_id=1, source_target_pairs={{0,16},{16,32},{32,48},{48,64},{64,80},{80,96},{96,112},{1,17},{17... | collective-permute-start | bytes 393224 | tf_op jit(solution)/shard_map/while/body/eval_jaxpr/ppermute | solution.py:16
  578.5 0.7 copy-start.1
  579.2 7.7 %collective-permute-start = (f32[8,64,64]{2,1,0:T(8,128)S(1)}, f32[8,64,64]{2,1,0:T(8,128)S(1)}, u32[]{:S(2)}, u32[]{:S(2)}) collective-permute-start(f32[8,64,64]{2,1,0:T(8,128)S(1)} %get-tuple-element.428), channel_id=1, source_target_pairs={{0,16},{16,32},{32,48},{48,64},{64,80},{80,96},{96,112},{1,17},{17... | collective-permute-start | bytes 393224 | tf_op jit(solution)/shard_map/while/body/eval_jaxpr/ppermute | solution.py:16
  586.9 0.7 copy-start.1
  590.5 1.9 copy-start.6
  590.5 2.2 copy-start.3
  590.5 2.2 copy-start.14
Sparse Core Ops, SparseCore 0:
  147.1 205.2 all-gather.1
  390.0 86.9 all-reduce.2
where the time goes:
time: 615 us; the launch traced here: 614 us
  waiting for transfers between devices  330 us (54%)
  blocking collectives  75.3 us (12%)
  starting transfers between devices  54.6 us (9%)
  local copies, waits for them, and re-layouts  52.2 us (8%)
  matrix products  46.7 us (8%)
  other arithmetic  41.4 us (7%)
  between operations  13.8 us (2%)
    all_gather x1, waiting for transfers between devices, shards(): lax.all_gather(normed, 'exp', axis=0, tiled=True)  205 us
    all_to_all x1, waiting for transfers between devices, shards(): lax.all_to_all(expert_rows, 'exp', split_axis=2, concat_axis=1, tiled=True)  100 us
    psum x1, blocking collectives, shards(): state_proj, dt_raw = lax.psum((state_part, rate_part), 'exp')  75.3 us
    ppermute x8, starting transfers between devices, passed_along(): lax.ppermute(value, axis, [(source, source + steps) for source in range(l...  46.7 us
    dot_general x1, matrix products, shards(): jnp.dot(lax.all_gather(normed, 'exp', axis=0, tiled=True), in_weight, pre...  23.7 us
    ppermute x8, waiting for transfers between devices, passed_along(): lax.ppermute(value, axis, [(source, source + steps) for source in range(l...  23.7 us
    gather x2, local copies, waits for them, and re-layouts, shards(): picked = jnp.take(buffers, expert_ids * capacity + expert_slots, axis=0)  20.2 us
    dot_general x8, matrix products, block_terms(): jnp.einsum('tsh,shp->thp', mixing, values, preferred_element_type=jnp.flo...  12.5 us
  transfers between devices with their start and end apart: 11, of which 11 were waited for; matrix products, arithmetic and copies ran while one was open for 2% of the time, Pallas kernels for 0%

commit v1 on v0

--- a/solution.py
+++ b/solution.py
@@ -8,6 +8,14 @@
 HEAD = 64
 NSTATE = 64
 STRETCH = 256
+
+
+def wrap_slots_now(sample):
+    res = tuple((sample for _ in range(lax.axis_size("exp"))))
+    after = jnp.stack(res, 0)
+    z1 = lax.all_to_all(after, "exp", split_axis=0, concat_axis=0)
+    val = jnp.concatenate(z1, 0)
+    return val
 
 
 def passed_along(value, axis, steps):
@@ -67,11 +75,9 @@
     normed = (stream * factor * norm_gain[None, :]).astype(jnp.bfloat16)
     group_rows = own_rows * lax.axis_size("exp")
     local_width = in_weight.shape[1]
-    x_in = jnp.dot(
-        lax.all_gather(normed, "exp", axis=0, tiled=True),
-        in_weight,
-        preferred_element_type=jnp.float32,
-    ).astype(jnp.bfloat16)
+    x_in = jnp.dot(wrap_slots_now(normed), in_weight, preferred_element_type=jnp.float32).astype(
+        jnp.bfloat16
+    )
     rim_rows = passed_along(x_in[group_rows - (KCONV - 1) :], "seq", 1)
     padded = jnp.concatenate([rim_rows, x_in], axis=0)
     filtered = jnp.zeros((group_rows, local_width), jnp.float32) + conv_bias[None, :]

time: 615 us -> 1050 us (1.71)
  waiting for transfers between devices: 330 us -> 741 us
  local copies, waits for them, and re-layouts: 52.2 us -> 63.1 us
    all_to_all x0 -> x1, waiting for transfers between devices: none -> 611 us  [wrap_slots_now(): z1 = lax.all_to_all(after, 'exp', split_axis=0, concat_axis=0)]
    all_gather x1 -> x0, waiting for transfers between devices: 205 us -> none  [shards(): lax.all_gather(normed, 'exp', axis=0, tiled=True)]
    all_to_all x0 -> x1, starting transfers between devices: none -> 11.5 us  [wrap_slots_now(): z1 = lax.all_to_all(after, 'exp', split_axis=0, concat_axis=0)]
    another operation x8 -> x9, local copies, waits for them, and re-layouts: 0.04 us -> 11 us  [the longest x1 11 us: wrap_slots_now(): after = jnp.stack(res, 0)]
  transfers between devices with their start and end apart: 11 -> 11, of which waited for: 11 -> 11; matrix products, arithmetic and copies ran while one was open for 2% -> 1% of each run, Pallas kernels for 0% -> 0%
where the time goes in v1:
time: 1050 us; the launch traced here: 1040 us
  waiting for transfers between devices  741 us (71%)
  blocking collectives  75.4 us (7%)
  starting transfers between devices  64.2 us (6%)
  local copies, waits for them, and re-layouts  63.1 us (6%)
  matrix products  46.7 us (4%)
  other arithmetic  40.2 us (4%)
  between operations  13.8 us (1%)
    all_to_all x1, waiting for transfers between devices, wrap_slots_now(): z1 = lax.all_to_all(after, 'exp', split_axis=0, concat_axis=0)  611 us
    all_to_all x1, waiting for transfers between devices, shards(): lax.all_to_all(expert_rows, 'exp', split_axis=2, concat_axis=1, tiled=True)  100 us
    psum x1, blocking collectives, shards(): state_proj, dt_raw = lax.psum((state_part, rate_part), 'exp')  75.4 us
    ppermute x8, starting transfers between devices, passed_along(): lax.ppermute(value, axis, [(source, source + steps) for source in range(l...  44.9 us
    dot_general x1, matrix products, shards(): jnp.dot(wrap_slots_now(normed), in_weight, preferred_element_type=jnp.flo...  23.8 us
    ppermute x8, waiting for transfers between devices, passed_along(): lax.ppermute(value, axis, [(source, source + steps) for source in range(l...  23.7 us
  transfers between devices with their start and end apart: 11, of which 11 were waited for; matrix products, arithmetic and copies ran while one was open for 1% of the time, Pallas kernels for 0%

profile of v1, /device:TPU:1, one launch (start us, length us, event | category | flops | bytes accessed | tf_op | source)
XLA Modules:
  0.0 1044.1 jit_solution(3027487828030560760)
XLA Ops:
  6.5 7.8 all-to-all-start
  14.6 100.5 %all-to-all-done = bf16[1,1,16,24,8192]{4,3,1,0,2:T(8,128)(2,1)} async-done(((bf16[1,1,16,24,8192]{4,3,1,0,2:T(8,128)(2,1)}), bf16[1,1,16,24,8192]{4,3,1,0,2:T(8,128)(2,1)}, u32[]{:S(2)}, u32[]{:S(2)}) %all-to-all-start) | async-done | bytes 6291488 | tf_op jit(solution)/shard_map/all_to_all | solution.py:64
  115.1 12.6 %gather_fusion = bf16[256,8192]{1,0:T(8,128)(2,1)} fusion(bf16[384,8192]{1,0:T(8,128)(2,1)} %bitcast.3, s32[1024]{0:T(1024)S(1)} %pad_clamp_fusion), kind=kCustom, calls=%fused_computation | custom fusion | bytes 8389632 | tf_op jit(solution)/shard_map/jit(_take)/gather | solution.py:67
  127.7 7.6 reshape.100
  135.3 7.2 copy_select_fusion
  142.5 1.4 multiply_reduce_fusion
  143.9 1.8 multiply_convert_fusion.1
  145.7 11.0 %stack.2 = bf16[16,128,8192]{2,1,0:T(8,128)(2,1)} broadcast(bf16[128,8192]{1,0:T(8,128)(2,1)S(1)} %multiply_convert_fusion.1), dimensions={1,2} | broadcast | bytes 35651584 | tf_op jit(solution)/shard_map/stack | solution.py:15
  156.7 11.5 %all-to-all-start.1 = ((bf16[16,128,8192]{2,1,0:T(8,128)(2,1)}), bf16[16,128,8192]{2,1,0:T(8,128)(2,1)}, u32[]{:S(2)}, u32[]{:S(2)}) async-start(bf16[16,128,8192]{2,1,0:T(8,128)(2,1)} %stack.2), calls=%async_computation.1 | async-start | bytes 67108864 | tf_op jit(solution)/shard_map/all_to_all | solution.py:16
  168.2 611.0 %all-to-all-done.1 = bf16[16,128,8192]{2,1,0:T(8,128)(2,1)} async-done(((bf16[16,128,8192]{2,1,0:T(8,128)(2,1)}), bf16[16,128,8192]{2,1,0:T(8,128)(2,1)}, u32[]{:S(2)}, u32[]{:S(2)}) %all-to-all-start.1) | async-done | bytes 33554464 | tf_op jit(solution)/shard_map/all_to_all | solution.py:16
  779.3 23.8 %convolution_convert_fusion = bf16[2048,512]{1,0:T(8,128)(2,1)S(1)} fusion(bf16[2048,8192]{1,0:T(8,128)(2,1)} %bitcast.7, bf16[8192,512]{1,0:T(8,128)(2,1)} %param.24), kind=kOutput, calls=%fused_computation.52 | convolution fusion | flops 17180917760 | bytes 44040192 | tf_op jit(solution)/shard_map/dot_general | solution.py:78
  804.4 6.5 collective-permute-start.1
  811.6 6.0 multiply_convert_fusion
  817.6 1.8 fusion.34
  819.5 1.7 fusion.35
  821.2 3.6 reshape.115
  824.8 4.0 copy.57
  828.8 75.4 %all-reduce.4 = bf16[2048,128]{1,0:T(8,128)(2,1)S(1)} all-reduce(f32[2048,128]{1,0:T(8,128)} %fusion.35), channel_id=1, replica_groups=mesh['seq'=8,'exp'=16] {'exp'}, use_global_device_ids=true, to_apply=%region_1.2 | all-reduce | flops 262144 | bytes 1572864 | tf_op jit(solution)/shard_map/psum | solution.py:91
  906.4 5.3 all-reduce.3.cloned.1.call-done
  912.7 38.5 %while.34 = (s32[]{:T(128)}, f32[8,64,64]{1,2,0:T(8,128)S(1)}, f32[8]{0:T(128)S(1)}, f32[8,256,8]{1,2,0:T(8,128)}, f32[8,256,8,64]{1,3,2,0:T(8,128)}, /*index=5*...) while((s32[]{:T(128)}, f32[8,64,64]{1,2,0:T(8,128)S(1)}, ...), condition=%wide.region_6.7_spmd.clone, body=%wide.region_3.6_spmd.clone.sunk | while | flops 180033568 | bytes 2758157 | solution.py:117
  914.0 1.6 fusion.62
  918.8 1.6 fusion.62
  923.6 1.6 fusion.62
  928.5 1.6 fusion.62
  933.3 1.6 fusion.62
  938.1 1.6 fusion.62
  942.9 1.6 fusion.62
  947.7 1.5 fusion.62
  951.4 66.4 %while.33 = (s32[]{:T(128)}, f32[8,64,64]{2,1,0:T(8,128)}, f32[8,64,64]{2,1,0:T(8,128)S(1)}, f32[8]{0:T(128)S(1)}, f32[8,64,64]{2,1,0:T(8,128)S(1)}, /*index=5*/s32[]{:T(128)}) while((s32[]{:T(128)}, f32[8,64,64]{2,1,0:T(8,128)}, f32[8,64,64]{2,1,0:T(8,128)S(1)}, f32[8]{0:T(128)S(1)}, f32[8,64,64]{2,1,0:T(8,128)S(1)}, ...), condition=%wide.region_8.9_spmd, body=%wide.region_7.8_spmd.sunk | while | flops 65538 | bytes 1441961 | solution.py:135
  951.4 12.2 %collective-permute-start = (f32[8,64,64]{2,1,0:T(8,128)S(1)}, f32[8,64,64]{2,1,0:T(8,128)S(1)}, u32[]{:S(2)}, u32[]{:S(2)}) collective-permute-start(f32[8,64,64]{2,1,0:T(8,128)S(1)} %get-tuple-element.428), channel_id=1, source_target_pairs={{0,16},{16,32},{32,48},{48,64},{64,80},{80,96},{96,112},{1,17},{17... | collective-permute-start | bytes 393224 | tf_op jit(solution)/shard_map/while/body/eval_jaxpr/ppermute | solution.py:24
  963.6 3.3 collective-permute-done
  967.6 4.4 collective-permute-start
  971.9 3.3 collective-permute-done
  975.9 4.4 collective-permute-start
  980.3 3.3 collective-permute-done
  984.3 4.4 collective-permute-start
  988.7 3.3 collective-permute-done
  992.7 4.4 collective-permute-start
  997.0 3.3 collective-permute-done
  1001.0 4.4 collective-permute-start
  1005.4 3.3 collective-permute-done
  1009.4 4.4 collective-permute-start
  1013.8 3.3 collective-permute-done
  1018.8 1.8 multiply_add_fusion.1
  1020.7 1.8 fusion.36
  1022.9 2.8 add_convert_fusion
  1025.7 5.1 copy.67
  1030.8 6.4 reshape.114
  (197 shorter events, 37.7 us)
Async XLA Ops:
  6.5 811.1 %copy-start = (bf16[512,128]{1,0:T(8,128)(2,1)S(1)}, bf16[512,128]{1,0:T(8,128)(2,1)}, u32[]{:S(2)}) copy-start(bf16[512,128]{1,0:T(8,128)(2,1)} %param.28) | copy-start | bytes 393220
  6.5 7.8 copy-start.10
  6.5 7.8 copy-start.11
  6.5 8.1 copy-start.12
  6.5 108.6 %all-to-all-start = ((bf16[1,1,16,24,8192]{4,3,1,0,2:T(8,128)(2,1)}), bf16[1,1,16,24,8192]{4,3,1,0,2:T(8,128)(2,1)}, u32[]{:S(2)}, u32[]{:S(2)}) async-start(bf16[1,1,16,24,8192]{4,3,1,0,2:T(8,128)(2,1)} %bitcast.114), calls=%async_computation | async-start | bytes 12582912 | tf_op jit(solution)/shard_map/all_to_all | solution.py:64
  135.3 7.2 copy-start.2
  142.5 1.4 copy-start.7
  156.7 11.5 %copy-start.8 = (f32[4,512]{1,0:T(4,128)S(1)}, f32[4,512]{1,0:T(4,128)}, u32[]{:S(2)}) copy-start(f32[4,512]{1,0:T(4,128)} %param.25) | copy-start | bytes 24580
  156.7 622.6 %all-to-all-start.1 = ((bf16[16,128,8192]{2,1,0:T(8,128)(2,1)}), bf16[16,128,8192]{2,1,0:T(8,128)(2,1)}, u32[]{:S(2)}, u32[]{:S(2)}) async-start(bf16[16,128,8192]{2,1,0:T(8,128)(2,1)} %stack.2), calls=%async_computation.1 | async-start | bytes 67108864 | tf_op jit(solution)/shard_map/all_to_all | solution.py:16
  168.2 743.5 %all-reduce.3.cloned.1.call-start = ((), (), s32[]{:S(2)}) async-start(), calls=%async_computation.2 | async-start | bytes 2097152 | tf_op jit(solution)/shard_map/psum | solution.py:91
  779.3 31.6 %copy-start.15 = (f32[8]{0:T(128)S(1)}, f32[8]{0:T(128)}, u32[]{:S(2)}) copy-start(f32[8]{0:T(128)} %param.30) | copy-start | bytes 100
  779.3 32.3 %copy-start.9 = (f32[512]{0:T(512)S(1)}, f32[512]{0:T(512)}, u32[]{:S(2)}) copy-start(f32[512]{0:T(512)} %param.26) | copy-start | bytes 6148
  803.1 1.3 copy-start.4
  804.4 7.2 collective-permute-start.1
  811.6 7.8 copy-start.5
  824.8 86.9 %copy-start.13 = (f32[8]{0:T(128)S(1)}, f32[8]{0:T(128)}, u32[]{:S(2)}) copy-start(f32[8]{0:T(128)} %param.29) | copy-start | bytes 100
  951.4 15.5 %collective-permute-start = (f32[8,64,64]{2,1,0:T(8,128)S(1)}, f32[8,64,64]{2,1,0:T(8,128)S(1)}, u32[]{:S(2)}, u32[]{:S(2)}) collective-permute-start(f32[8,64,64]{2,1,0:T(8,128)S(1)} %get-tuple-element.428), channel_id=1, source_target_pairs={{0,16},{16,32},{32,48},{48,64},{64,80},{80,96},{96,112},{1,17},{17... | collective-permute-start | bytes 393224 | tf_op jit(solution)/shard_map/while/body/eval_jaxpr/ppermute | solution.py:24
  966.9 0.7 copy-start.1
  967.6 7.7 collective-permute-start
  975.2 0.7 copy-start.1
  975.9 7.7 collective-permute-start
  983.6 0.7 copy-start.1
  984.3 7.7 collective-permute-start
  992.0 0.7 copy-start.1
  992.7 7.7 collective-permute-start
  1000.3 0.7 copy-start.1
  1001.0 7.7 collective-permute-start
  1008.7 0.7 copy-start.1
  1009.4 7.7 collective-permute-start
  1017.1 0.7 copy-start.1
  1020.7 1.9 copy-start.6
  1020.7 2.2 copy-start.3
  1020.7 2.2 copy-start.14
Sparse Core Ops, SparseCore 0:
  819.6 92.0 all-reduce.2
